TPU v7x, 32 devices: a whole 2x2x4 slice. The times are simulated.
32 devices in a mesh: rep: 2 (over core), grp: 16 (over z, y, x).
Axes of the slice: x: 2, y: 2, z: 4, core: 2. Of those that a mesh axis runs over, the one named last changes fastest.
Arguments:
- grad_parts: float32 [2, 1024, 9216], P('rep', 'grp'), may hold values from -6 to 6
- gain_grad_parts: float32 [2, 2, 1024], P('rep', None, 'grp'), may hold values from -6 to 6
- weights: float32 [1024, 9216], P('grp'), may hold values from -0.1875 to 0.1875
- basis: float32 [1024, 256], P('grp'), may hold values from -0.1875 to 0.1875
- moment_first: float32 [9216, 256], P('grp'), may hold values from -12 to 12
- moment_second: float32 [9216, 256], P('grp'), may hold values from 0.01 to 1
- gains: float32 [2, 1024], P(None, 'grp'), may hold values from 0.5 to 1.5
- gain_first: float32 [2, 1024], P(None, 'grp'), may hold values from -12 to 12
- gain_second: float32 [2, 1024], P(None, 'grp'), may hold values from 0.01 to 1
Outputs:
- new_weights: float32 [1024, 9216], P('grp')
- new_first: float32 [9216, 256], P('grp')
- new_second: float32 [9216, 256], P('grp')
- new_basis: float32 [1024, 256], P('grp')
- new_gains: float32 [2, 1024], P(None, 'grp')
- new_gain_first: float32 [2, 1024], P(None, 'grp')
- new_gain_second: float32 [2, 1024], P(None, 'grp')
All inputs are finite; a program needn't handle non-finite values.
Results may differ from a plain program's by a relative error of at most 0.0001.
Values sent between devices are 32-bit elements; how exact they have to be, the bound alone decides.
A program may use at most 64 MiB of HBM per device.

v0:
```python
import jax
import jax.numpy as jnp
from jax import lax
from jax.sharding import PartitionSpec as P

NS_STEPS = 3
beta_first = 0.9
beta_second = 0.999
learn_rate = 0.1
galore_scale = 0.25
adam_eps = 1e-08


def exact_dot(left, right):
    return jnp.dot(left, right, precision=lax.Precision.HIGHEST, preferred_element_type=jnp.float32)


def body(
    grad_parts,
    gain_grad_parts,
    weights,
    basis,
    moment_first,
    moment_second,
    gains,
    gain_first,
    gain_second,
):
    corr_first = 1.0 - beta_first**10
    corr_second = 1.0 - beta_second**10
    n = lax.axis_size("grp")
    rep = lax.axis_index("rep")
    swap = [(0, 1), (1, 0)]
    local_grad = grad_parts[0]
    local_gain = gain_grad_parts[0]
    rows, ncol = local_grad.shape
    half = rows // 2
    block = ncol // n
    rank = basis.shape[1]

    def own_half(x):
        return lax.dynamic_slice_in_dim(x, rep * half, half, 0)

    def other_half(x):
        return lax.dynamic_slice_in_dim(x, (1 - rep) * half, half, 0)

    def swapped(x):
        return lax.ppermute(x, "rep", swap)

    def joined(mine, other):
        return jnp.where(
            rep == 0, jnp.concatenate([mine, other], 0), jnp.concatenate([other, mine], 0)
        )

    def exchange(x):
        return lax.all_to_all(x, "grp", split_axis=0, concat_axis=0, tiled=True)

    def gathered(x):
        return exchange(jnp.tile(x, (n, 1)))

    half_basis = gathered(own_half(basis))
    source = own_half(local_grad) + swapped(other_half(local_grad))
    gain_grad = local_gain + swapped(local_gain)
    col_block = lax.all_to_all(source, "grp", split_axis=1, concat_axis=0, tiled=True)
    partial = exact_dot(col_block.T, half_basis)
    projected = partial + swapped(partial)
    new_first = beta_first * moment_first + (1.0 - beta_first) * projected
    new_second = beta_second * moment_second + (1.0 - beta_second) * projected * projected
    direction = new_first / corr_first / (jnp.sqrt(new_second / corr_second) + adam_eps)
    terms = exchange(exact_dot(col_block, projected))
    sub_half = jnp.sum(terms.reshape(n, half, rank), axis=0)
    sub_all = gathered(sub_half)
    gram_half = exact_dot(sub_all.T, sub_all)
    gram = gram_half + swapped(gram_half)
    subspace = joined(sub_half, swapped(sub_half))
    update_cols = exact_dot(half_basis, direction.T)
    update = lax.all_to_all(update_cols, "grp", split_axis=0, concat_axis=1, tiled=True)
    new_half = own_half(weights) - learn_rate * galore_scale * update
    new_weights = joined(new_half, swapped(new_half))
    scale = jnp.sqrt(jnp.sqrt(jnp.sum(gram * gram) + 1e-06))
    iterate = subspace / scale
    current = gram / scale / scale
    for step in range(NS_STEPS):
        iterate = 1.5 * iterate - 0.5 * exact_dot(iterate, current)
        if step + 1 < NS_STEPS:
            side = 1.5 * current - 0.5 * exact_dot(current, current)
            current = 1.5 * side - 0.5 * exact_dot(side, current)
    new_gain_first = beta_first * gain_first + (1.0 - beta_first) * gain_grad
    new_gain_second = beta_second * gain_second + (1.0 - beta_second) * gain_grad * gain_grad
    new_gains = gains - learn_rate * (new_gain_first / corr_first) / (
        jnp.sqrt(new_gain_second / corr_second) + adam_eps
    )
    return (new_weights, new_first, new_second, iterate, new_gains, new_gain_first, new_gain_second)


def solution(mesh):
    in_specs = (
        P("rep", "grp", None),
        P("rep", None, "grp"),
        P("grp", None),
        P("grp", None),
        P("grp", None),
        P("grp", None),
        P(None, "grp"),
        P(None, "grp"),
        P(None, "grp"),
    )
    out_specs = (
        P("grp", None),
        P("grp", None),
        P("grp", None),
        P("grp", None),
        P(None, "grp"),
        P(None, "grp"),
        P(None, "grp"),
    )
    return jax.shard_map(body, mesh=mesh, in_specs=in_specs, out_specs=out_specs, check_vma=False)
```

profile of v0, /device:TPU:9, one launch (start us, length us, event | category | flops | bytes accessed | tf_op | source)
XLA Modules:
  0.0 149.2 jit_solution(4049808414563732338)
XLA Ops:
  0.6 0.0 copy-start
  0.7 1.4 dynamic-slice_bitcast_fusion
  2.0 0.7 collective-permute-start
  2.8 0.0 copy-done
  2.8 0.8 tile.4
  3.6 6.7 %all-to-all-start = ((f32[16,32,256]{2,1,0:T(8,128)}), f32[16,32,256]{2,1,0:T(8,128)S(1)}, u32[]{:S(2)}, u32[]{:S(2)}) async-start(f32[16,32,256]{2,1,0:T(8,128)} %tile.4), calls=%async_computation | async-start | bytes 1048576 | tf_op jit(solution)/shard_map/all_to_all | solution.py:56
  10.3 0.0 collective-permute-done
  10.3 1.4 bitcast_add_fusion
  11.7 0.4 all_to_all.33
  12.2 0.4 copy.16
  12.6 11.6 %all-to-all-done = f32[16,32,256]{2,1,0:T(8,128)S(1)} async-done(((f32[16,32,256]{2,1,0:T(8,128)}), f32[16,32,256]{2,1,0:T(8,128)S(1)}, u32[]{:S(2)}, u32[]{:S(2)}) %all-to-all-start) | async-done | bytes 524320 | tf_op jit(solution)/shard_map/all_to_all | solution.py:56
  24.2 0.0 copy-start.3
  24.2 35.0 %all_to_all.44 = f32[32,16,576]{2,0,1:T(8,128)S(1)} all-to-all(f32[32,16,576]{2,0,1:T(8,128)S(1)} %copy.16), channel_id=1, replica_groups=mesh['rep'=2,'grp'=16] {'grp'}, dimensions={1} | all-to-all | bytes 2359296 | tf_op jit(solution)/shard_map/all_to_all | solution.py:64
  59.2 0.0 copy-done.3
  59.2 2.2 %fusion.4 = f32[576,256]{1,0:T(8,128)S(1)} fusion(f32[16,32,256]{2,1,0:T(8,128)S(1)} %all-to-all-done, f32[32,16,576]{2,0,1:T(8,128)S(1)} %all_to_all.44), kind=kOutput, calls=%fused_computation.6 | convolution fusion | flops 905969664 | bytes 2293760 | tf_op jit(solution)/shard_map/dot_general | solution.py:15
  61.5 2.0 %collective-permute-start.1 = (f32[576,256]{1,0:T(8,128)S(1)}, f32[576,256]{1,0:T(8,128)S(1)}, u32[]{:S(2)}, u32[]{:S(2)}) collective-permute-start(f32[576,256]{1,0:T(8,128)S(1)} %fusion.4), channel_id=1, source_target_pairs={{0,16},{16,0},{1,17},{17,1},{2,18},{18,2},{3,19},{19,3},{4,20},{20... | collective-permute-start | bytes 1769480 | tf_op jit(solution)/shard_map/ppermute | solution.py:48
  63.5 1.6 %collective-permute-done.1 = f32[576,256]{1,0:T(8,128)S(1)} collective-permute-done((f32[576,256]{1,0:T(8,128)S(1)}, f32[576,256]{1,0:T(8,128)S(1)}, u32[]{:S(2)}, u32[]{:S(2)}) %collective-permute-start.1) | collective-permute-done | bytes 589856 | tf_op jit(solution)/shard_map/ppermute | solution.py:48
  65.1 1.4 fusion
  66.5 17.3 %all_to_all.45 = f32[16,32,256]{2,1,0:T(8,128)S(1)} all-to-all(f32[16,32,256]{2,1,0:T(8,128)S(1)} %fusion), channel_id=1, replica_groups=mesh['rep'=2,'grp'=16] {'grp'}, dimensions={0} | all-to-all | bytes 1048576 | tf_op jit(solution)/shard_map/all_to_all | solution.py:56
  83.8 0.0 copy-start.5
  83.9 0.8 tile.5
  84.7 4.6 %all-to-all-start.4 = ((f32[16,32,256]{2,1,0:T(8,128)}), f32[16,32,256]{2,1,0:T(8,128)}, u32[]{:S(2)}, u32[]{:S(2)}) async-start(f32[16,32,256]{2,1,0:T(8,128)} %tile.5), calls=%async_computation.4 | async-start | bytes 1048576 | tf_op jit(solution)/shard_map/all_to_all | solution.py:56
  89.4 0.0 copy-done.5
  89.4 0.0 copy-start.4
  89.4 1.3 multiply_add_fusion
  90.7 0.0 copy-start.2
  90.7 0.0 copy-start.1
  90.7 0.8 copy-done.2
  91.5 0.0 copy-done.4
  91.5 2.7 %fusion.13 = f32[16,32,576]{2,1,0:T(8,128)} fusion(f32[16,32,256]{2,1,0:T(8,128)S(1)} %copy-done.4, f32[576,256]{1,0:T(8,128)S(1)} %get-tuple-element.13, f32[576,256]{1,0:T(8,128)S(1)} %get-tuple-element.12), kind=kOutput, calls=%fused_computation.25 | convolution fusion | flops 906559488 | bytes 2883584 | tf_op jit(solution)/shard_map/dot_general | solution.py:15
  94.3 0.0 copy-done.1
  94.3 0.0 copy-start.7
  94.3 0.0 copy-start.6
  94.3 0.0 copy-start.9
  94.3 8.3 %all-to-all-done.4 = f32[16,32,256]{2,1,0:T(8,128)} async-done(((f32[16,32,256]{2,1,0:T(8,128)}), f32[16,32,256]{2,1,0:T(8,128)}, u32[]{:S(2)}, u32[]{:S(2)}) %all-to-all-start.4) | async-done | bytes 524320 | tf_op jit(solution)/shard_map/all_to_all | solution.py:56
  102.6 5.1 %all-to-all-start.2 = ((f32[16,32,576]{2,1,0:T(8,128)}), f32[16,32,576]{2,1,0:T(8,128)S(1)}, u32[]{:S(2)}, u32[]{:S(2)}) async-start(f32[16,32,576]{2,1,0:T(8,128)} %fusion.13), calls=%async_computation.2 | async-start | bytes 2621440 | tf_op jit(solution)/shard_map/all_to_all | solution.py:77
  107.6 0.0 copy-done.7
  107.6 2.2 %collective-permute-start.5 = (f32[2,64]{1,0:T(2,128)S(1)}, f32[2,64]{1,0:T(2,128)S(1)}, u32[]{:S(2)}, u32[]{:S(2)}) collective-permute-start(f32[2,64]{1,0:T(2,128)S(1)} %bitcast.39), channel_id=1, source_target_pairs={{0,16},{16,0},{1,17},{17,1},{2,18},{18,2},{3,19},{19,3},{4,20},{20... | collective-permute-start | bytes 1544 | tf_op jit(solution)/shard_map/ppermute | solution.py:48
  109.8 0.8 collective-permute-done.5
  110.6 0.0 copy-done.6
  110.6 0.0 copy-done.8
  110.6 0.0 copy-done.9
  110.6 0.6 divide_subtract_fusion
  111.2 0.3 collective-permute-start.3
  111.6 2.2 %convolution_bitcast_fusion = f32[256,256]{1,0:T(8,128)S(1)} fusion(f32[16,32,256]{2,1,0:T(8,128)} %all-to-all-done.4), kind=kOutput, calls=%fused_computation.16 | convolution fusion | flops 402653184 | bytes 786432 | tf_op jit(solution)/shard_map/dot_general | solution.py:15
  113.8 0.2 collective-permute-start.4
  114.0 23.7 %all-to-all-done.2 = f32[16,32,576]{2,1,0:T(8,128)S(1)} async-done(((f32[16,32,576]{2,1,0:T(8,128)}), f32[16,32,576]{2,1,0:T(8,128)S(1)}, u32[]{:S(2)}, u32[]{:S(2)}) %all-to-all-start.2) | async-done | bytes 1179680 | tf_op jit(solution)/shard_map/all_to_all | solution.py:77
  137.8 0.1 multiply_bitcast_fusion
  137.9 0.8 copy.17
  138.7 0.5 mul.135
  139.1 1.4 dynamic-slice_subtract_fusion
  140.5 2.6 %collective-permute-start.2 = (f32[32,9216]{1,0:T(8,128)S(1)}, f32[32,9216]{1,0:T(8,128)S(1)}, u32[]{:S(2)}, u32[]{:S(2)}) collective-permute-start(f32[32,9216]{1,0:T(8,128)S(1)} %dynamic-slice_subtract_fusion), channel_id=1, source_target_pairs={{0,16},{16,0},{1,17},{17,1},{2,18},{18,2},{3,19},{19,3},{4,20},{20... | collective-permute-start | bytes 3538952 | tf_op jit(solution)/shard_map/ppermute | solution.py:48
  143.2 0.0 collective-permute-done.4
  143.2 0.7 multiply_reduce_fusion
  144.6 0.4 convolution_multiply_fusion.3
  145.0 0.4 multiply_subtract_fusion
  145.4 0.0 collective-permute-done.3
  145.4 0.3 convolution_multiply_fusion.6
  145.7 0.3 fusion.10
  145.9 0.4 fusion.8
  146.3 0.4 fusion.7
  146.7 0.9 fusion.9
  147.6 0.0 collective-permute-done.2
  147.6 1.6 %maximum_select_fusion = f32[64,9216]{1,0:T(8,128)} fusion(f32[32,9216]{1,0:T(8,128)S(1)} %collective-permute-done.2, f32[32,9216]{1,0:T(8,128)S(1)} %dynamic-slice_subtract_fusion, pred[]{:T(512)S(6)} %eq.4), kind=kLoop, calls=%fused_computation | loop fusion | flops 1769472 | bytes 4718593 | tf_op jit(solution)/shard_map/jit(_where)/select_n | solution.py:51
  (3 shorter events, 0.0 us)
Async XLA Ops:
  0.6 2.2 %copy-start = (f32[64,256]{1,0:T(8,128)S(1)}, f32[64,256]{1,0:T(8,128)}, u32[]{:S(2)}) copy-start(f32[64,256]{1,0:T(8,128)} %param.12) | copy-start | bytes 196612
  2.0 8.3 %collective-permute-start = (f32[32,9216]{1,0:T(8,128)S(1)}, f32[32,9216]{1,0:T(8,128)S(1)}, u32[]{:S(2)}, u32[]{:S(2)}) collective-permute-start(f32[32,9216]{1,0:T(8,128)S(1)} %dynamic-slice_bitcast_fusion), channel_id=1, source_target_pairs={{0,16},{16,0},{1,17},{17,1},{2,18},{18,2},{3,19},{19,3},{4,20},{20... | collective-permute-start | bytes 3538952 | tf_op jit(solution)/shard_map/ppermute | solution.py:48
  3.6 20.6 %all-to-all-start = ((f32[16,32,256]{2,1,0:T(8,128)}), f32[16,32,256]{2,1,0:T(8,128)S(1)}, u32[]{:S(2)}, u32[]{:S(2)}) async-start(f32[16,32,256]{2,1,0:T(8,128)} %tile.4), calls=%async_computation | async-start | bytes 1048576 | tf_op jit(solution)/shard_map/all_to_all | solution.py:56
  24.2 35.0 %copy-start.3 = (f32[16,32,256]{2,1,0:T(8,128)}, f32[16,32,256]{2,1,0:T(8,128)S(1)}, u32[]{:S(2)}) copy-start(f32[16,32,256]{2,1,0:T(8,128)S(1)} %all-to-all-done) | copy-start | bytes 1572868
  61.5 3.6 %collective-permute-start.1 = (f32[576,256]{1,0:T(8,128)S(1)}, f32[576,256]{1,0:T(8,128)S(1)}, u32[]{:S(2)}, u32[]{:S(2)}) collective-permute-start(f32[576,256]{1,0:T(8,128)S(1)} %fusion.4), channel_id=1, source_target_pairs={{0,16},{16,0},{1,17},{17,1},{2,18},{18,2},{3,19},{19,3},{4,20},{20... | collective-permute-start | bytes 1769480 | tf_op jit(solution)/shard_map/ppermute | solution.py:48
  83.8 5.5 %copy-start.5 = (f32[576,256]{1,0:T(8,128)S(1)}, f32[576,256]{1,0:T(8,128)}, u32[]{:S(2)}) copy-start(f32[576,256]{1,0:T(8,128)} %param.13) | copy-start | bytes 1769476
  84.7 17.9 %all-to-all-start.4 = ((f32[16,32,256]{2,1,0:T(8,128)}), f32[16,32,256]{2,1,0:T(8,128)}, u32[]{:S(2)}, u32[]{:S(2)}) async-start(f32[16,32,256]{2,1,0:T(8,128)} %tile.5), calls=%async_computation.4 | async-start | bytes 1048576 | tf_op jit(solution)/shard_map/all_to_all | solution.py:56
  89.4 2.2 %copy-start.4 = (f32[16,32,256]{2,1,0:T(8,128)S(1)}, f32[16,32,256]{2,1,0:T(8,128)}, u32[]{:S(2)}) copy-start(f32[16,32,256]{2,1,0:T(8,128)} %copy-done.3) | copy-start | bytes 1572868
  90.7 0.8 copy-start.2
  90.7 3.6 %copy-start.1 = (f32[576,256]{1,0:T(8,128)}, f32[576,256]{1,0:T(8,128)S(1)}, u32[]{:S(2)}) copy-start(f32[576,256]{1,0:T(8,128)S(1)} %get-tuple-element.12) | copy-start | bytes 1769476
  94.3 13.4 %copy-start.7 = (f32[1,2,64]{2,1,0:T(2,128)S(1)}, f32[1,2,64]{2,1,0:T(2,128)}, u32[]{:S(2)}) copy-start(f32[1,2,64]{2,1,0:T(2,128)} %param.10) | copy-start | bytes 1540
  94.3 16.4 %copy-start.6 = (f32[2,64]{1,0:T(2,128)S(1)}, f32[2,64]{1,0:T(2,128)}, u32[]{:S(2)}) copy-start(f32[2,64]{1,0:T(2,128)} %param.15) | copy-start | bytes 1540
  94.3 16.4 %copy-start.8 = (f32[2,64]{1,0:T(2,128)S(1)}, f32[2,64]{1,0:T(2,128)}, u32[]{:S(2)}) copy-start(f32[2,64]{1,0:T(2,128)} %param.16) | copy-start | bytes 1540
  94.3 16.4 %copy-start.9 = (f32[2,64]{1,0:T(2,128)S(1)}, f32[2,64]{1,0:T(2,128)}, u32[]{:S(2)}) copy-start(f32[2,64]{1,0:T(2,128)} %param.17) | copy-start | bytes 1540
  102.6 35.2 %all-to-all-start.2 = ((f32[16,32,576]{2,1,0:T(8,128)}), f32[16,32,576]{2,1,0:T(8,128)S(1)}, u32[]{:S(2)}, u32[]{:S(2)}) async-start(f32[16,32,576]{2,1,0:T(8,128)} %fusion.13), calls=%async_computation.2 | async-start | bytes 2621440 | tf_op jit(solution)/shard_map/all_to_all | solution.py:77
  107.6 3.0 %collective-permute-start.5 = (f32[2,64]{1,0:T(2,128)S(1)}, f32[2,64]{1,0:T(2,128)S(1)}, u32[]{:S(2)}, u32[]{:S(2)}) collective-permute-start(f32[2,64]{1,0:T(2,128)S(1)} %bitcast.39), channel_id=1, source_target_pairs={{0,16},{16,0},{1,17},{17,1},{2,18},{18,2},{3,19},{19,3},{4,20},{20... | collective-permute-start | bytes 1544 | tf_op jit(solution)/shard_map/ppermute | solution.py:48
  111.2 34.2 %collective-permute-start.3 = (f32[32,256]{1,0:T(8,128)S(1)}, f32[32,256]{1,0:T(8,128)S(1)}, u32[]{:S(2)}, u32[]{:S(2)}) collective-permute-start(f32[32,256]{1,0:T(8,128)S(1)} %reduce_sum.18), channel_id=1, source_target_pairs={{0,16},{16,0},{1,17},{17,1},{2,18},{18,2},{3,19},{19,3},{4,20},{20... | collective-permute-start | bytes 98312 | tf_op jit(solution)/shard_map/ppermute | solution.py:48
  113.8 29.4 %collective-permute-start.4 = (f32[256,256]{1,0:T(8,128)S(1)}, f32[256,256]{1,0:T(8,128)S(1)}, u32[]{:S(2)}, u32[]{:S(2)}) collective-permute-start(f32[256,256]{1,0:T(8,128)S(1)} %convolution_bitcast_fusion), channel_id=1, source_target_pairs={{0,16},{16,0},{1,17},{17,1},{2,18},{18,2},{3,19},{19,3},{4,20},{20... | collective-permute-start | bytes 786440 | tf_op jit(solution)/shard_map/ppermute | solution.py:48
  140.5 7.1 %collective-permute-start.2 = (f32[32,9216]{1,0:T(8,128)S(1)}, f32[32,9216]{1,0:T(8,128)S(1)}, u32[]{:S(2)}, u32[]{:S(2)}) collective-permute-start(f32[32,9216]{1,0:T(8,128)S(1)} %dynamic-slice_subtract_fusion), channel_id=1, source_target_pairs={{0,16},{16,0},{1,17},{17,1},{2,18},{18,2},{3,19},{19,3},{4,20},{20... | collective-permute-start | bytes 3538952 | tf_op jit(solution)/shard_map/ppermute | solution.py:48
where the time goes:
time: 150 us; the launch traced here: 149 us
  blocking collectives  52.4 us (35%)
  waiting for transfers between devices  46.1 us (31%)
  starting transfers between devices  24.5 us (16%)
  matrix products  11.5 us (8%)
  other arithmetic  7.11 us (5%)
  local copies, waits for them, and re-layouts  6.02 us (4%)
  between operations  1.58 us (1%)
    all_to_all x1, blocking collectives, body(): lax.all_to_all(source, 'grp', split_axis=1, concat_axis=0, tiled=True)  35 us
    all_to_all x1, waiting for transfers between devices, body(): lax.all_to_all(update_cols, 'grp', split_axis=0, concat_axis=1, tiled=True)  23.7 us
    all_to_all x2, waiting for transfers between devices, exchange(): return lax.all_to_all(x, 'grp', split_axis=0, concat_axis=0, tiled=True)  19.9 us
    all_to_all x1, blocking collectives, exchange(): return lax.all_to_all(x, 'grp', split_axis=0, concat_axis=0, tiled=True)  17.3 us
    dot_general x11, matrix products, exact_dot(): jnp.dot(left, right, precision=lax.Precision.HIGHEST, preferred_element_t...  11.5 us
    all_to_all x2, starting transfers between devices, exchange(): return lax.all_to_all(x, 'grp', split_axis=0, concat_axis=0, tiled=True)  11.3 us
    ppermute x6, starting transfers between devices, swapped(): return lax.ppermute(x, 'rep', swap)  8.15 us
    all_to_all x1, starting transfers between devices, body(): lax.all_to_all(update_cols, 'grp', split_axis=0, concat_axis=1, tiled=True)  5.05 us
  transfers between devices with their start and end apart: 9, of which 5 were waited for; matrix products, arithmetic and copies ran while one was open for 11% of the time, Pallas kernels for 0%

commit v1 on v0

--- a/solution.py
+++ b/solution.py
@@ -74,7 +74,12 @@
     gram = gram_half + swapped(gram_half)
     subspace = joined(sub_half, swapped(sub_half))
     update_cols = exact_dot(half_basis, direction.T)
-    update = lax.all_to_all(update_cols, "grp", split_axis=0, concat_axis=1, tiled=True)
+    update = jnp.concatenate(
+        lax.all_to_all(
+            jnp.stack(jnp.split(update_cols, lax.axis_size("grp"), axis=0)), "grp", 0, 0
+        ),
+        axis=1,
+    )
     new_half = own_half(weights) - learn_rate * galore_scale * update
     new_weights = joined(new_half, swapped(new_half))
     scale = jnp.sqrt(jnp.sqrt(jnp.sum(gram * gram) + 1e-06))

time: 150 us -> 163 us (1.087)
  local copies, waits for them, and re-layouts: 6.02 us -> 31.2 us
  blocking collectives: 52.4 us -> 35 us
  starting transfers between devices: 24.5 us -> 30.1 us
  matrix products: 11.5 us -> 9.77 us
    all_to_all x1 -> x0, blocking collectives: 17.3 us -> none  [exchange(): return lax.all_to_all(x, 'grp', split_axis=0, concat_axis=0, tiled=True)]
    another operation x0 -> x18, local copies, waits for them, and re-layouts: none -> 15.5 us  [body(): jnp.stack(jnp.split(update_cols, lax.axis_size('grp'), axis=0))]
    unnamed x20 -> x51, local copies, waits for them, and re-layouts: 0.84 us -> 10.5 us
    all_to_all x2 -> x3, starting transfers between devices: 11.3 us -> 17.4 us  [exchange(): return lax.all_to_all(x, 'grp', split_axis=0, concat_axis=0, tiled=True)]
    dot_general x11, matrix products: 11.5 us -> 9.77 us  [exact_dot(): jnp.dot(left, right, precision=lax.Precision.HIGHEST, preferred_element_t...]
    all_to_all x2 -> x3, waiting for transfers between devices: 19.9 us -> 19.5 us  [exchange(): return lax.all_to_all(x, 'grp', split_axis=0, concat_axis=0, tiled=True)]
  transfers between devices with their start and end apart: 9 -> 10, of which waited for: 5 -> 5; matrix products, arithmetic and copies ran while one was open for 11% -> 24% of each run, Pallas kernels for 0% -> 0%
where the time goes in v1:
time: 163 us; the launch traced here: 162 us
  waiting for transfers between devices  47.1 us (29%)
  blocking collectives  35 us (21%)
  local copies, waits for them, and re-layouts  31.2 us (19%)
  starting transfers between devices  30.1 us (18%)
  matrix products  9.77 us (6%)
  other arithmetic  7.29 us (4%)
    all_to_all x1, blocking collectives, body(): lax.all_to_all(source, 'grp', split_axis=1, concat_axis=0, tiled=True)  35 us
    all_to_all x1, waiting for transfers between devices, body(): lax.all_to_all(jnp.stack(jnp.split(update_cols, lax.axis_size('grp'), axi...  25.1 us
    all_to_all x3, waiting for transfers between devices, exchange(): return lax.all_to_all(x, 'grp', split_axis=0, concat_axis=0, tiled=True)  19.5 us
    all_to_all x3, starting transfers between devices, exchange(): return lax.all_to_all(x, 'grp', split_axis=0, concat_axis=0, tiled=True)  17.4 us
    another operation x18, local copies, waits for them, and re-layouts, body(): jnp.stack(jnp.split(update_cols, lax.axis_size('grp'), axis=0))  15.5 us
    unnamed x51, local copies, waits for them, and re-layouts  10.5 us
    dot_general x11, matrix products, exact_dot(): jnp.dot(left, right, precision=lax.Precision.HIGHEST, preferred_element_t...  9.77 us
    ppermute x6, starting transfers between devices, swapped(): return lax.ppermute(x, 'rep', swap)  7.99 us
  transfers between devices with their start and end apart: 10, of which 5 were waited for; matrix products, arithmetic and copies ran while one was open for 24% of the time, Pallas kernels for 0%

profile of v1, /device:TPU:9, one launch (start us, length us, event | category | flops | bytes accessed | tf_op | source)
XLA Modules:
  0.0 162.1 jit_solution(6625808407353334620)
XLA Ops:
  0.7 1.4 dynamic-slice_bitcast_fusion
  2.0 0.7 collective-permute-start
  2.8 0.8 tile.4
  3.6 6.7 %all-to-all-start = ((f32[16,32,256]{2,1,0:T(8,128)}), f32[16,32,256]{2,1,0:T(8,128)S(1)}, u32[]{:S(2)}, u32[]{:S(2)}) async-start(f32[16,32,256]{2,1,0:T(8,128)} %tile.4), calls=%async_computation | async-start | bytes 1048576 | tf_op jit(solution)/shard_map/all_to_all | solution.py:56
  10.3 1.4 bitcast_add_fusion
  11.7 0.4 all_to_all.31
  12.2 0.4 copy.36
  12.6 11.6 %all-to-all-done = f32[16,32,256]{2,1,0:T(8,128)S(1)} async-done(((f32[16,32,256]{2,1,0:T(8,128)}), f32[16,32,256]{2,1,0:T(8,128)S(1)}, u32[]{:S(2)}, u32[]{:S(2)}) %all-to-all-start) | async-done | bytes 524320 | tf_op jit(solution)/shard_map/all_to_all | solution.py:56
  24.2 35.0 %all_to_all.42 = f32[32,16,576]{2,0,1:T(8,128)S(1)} all-to-all(f32[32,16,576]{2,0,1:T(8,128)S(1)} %copy.36), channel_id=1, replica_groups=mesh['rep'=2,'grp'=16] {'grp'}, dimensions={1} | all-to-all | bytes 2359296 | tf_op jit(solution)/shard_map/all_to_all | solution.py:64
  59.2 2.2 %fusion.4 = f32[576,256]{1,0:T(8,128)S(1)} fusion(f32[16,32,256]{2,1,0:T(8,128)S(1)} %all-to-all-done, f32[32,16,576]{2,0,1:T(8,128)S(1)} %all_to_all.42), kind=kOutput, calls=%fused_computation.6 | convolution fusion | flops 905969664 | bytes 2293760 | tf_op jit(solution)/shard_map/dot_general | solution.py:15
  61.5 2.0 %collective-permute-start.1 = (f32[576,256]{1,0:T(8,128)S(1)}, f32[576,256]{1,0:T(8,128)S(1)}, u32[]{:S(2)}, u32[]{:S(2)}) collective-permute-start(f32[576,256]{1,0:T(8,128)S(1)} %fusion.4), channel_id=1, source_target_pairs={{0,16},{16,0},{1,17},{17,1},{2,18},{18,2},{3,19},{19,3},{4,20},{20... | collective-permute-start | bytes 1769480 | tf_op jit(solution)/shard_map/ppermute | solution.py:48
  63.5 1.6 %collective-permute-done.1 = f32[576,256]{1,0:T(8,128)S(1)} collective-permute-done((f32[576,256]{1,0:T(8,128)S(1)}, f32[576,256]{1,0:T(8,128)S(1)}, u32[]{:S(2)}, u32[]{:S(2)}) %collective-permute-start.1) | collective-permute-done | bytes 589856 | tf_op jit(solution)/shard_map/ppermute | solution.py:48
  65.1 2.2 %fusion = f32[16,32,256]{2,1,0:T(8,128)} fusion(f32[32,16,576]{2,0,1:T(8,128)S(1)} %all_to_all.42, f32[576,256]{1,0:T(8,128)S(1)} %fusion.4, f32[576,256]{1,0:T(8,128)S(1)} %collective-permute-done.1), kind=kOutput, calls=%fused_computation.1 | convolution fusion | flops 906117120 | bytes 2883584 | tf_op jit(solution)/shard_map/dot_general | solution.py:15
  67.3 4.2 %all-to-all-start.3 = ((f32[16,32,256]{2,1,0:T(8,128)}), f32[16,32,256]{2,1,0:T(8,128)S(1)}, u32[]{:S(2)}, u32[]{:S(2)}) async-start(f32[16,32,256]{2,1,0:T(8,128)} %fusion), calls=%async_computation.3 | async-start | bytes 1048576 | tf_op jit(solution)/shard_map/all_to_all | solution.py:56
  71.5 1.5 multiply_add_fusion
  73.1 0.8 copy-done.2
  73.9 1.4 fusion.13
  75.2 2.3 %slice_bitcast_fusion = (f32[1,32,576]{1,2,0:T(8,128)}, f32[1,32,576]{1,2,0:T(8,128)}, f32[1,32,576]{1,2,0:T(8,128)}, f32[1,32,576]{1,2,0:T(8,128)}, f32[1,32,57...) fusion(f32[512,576]{0,1:T(8,128)S(1)} %fusion.13), kind=kLoop, calls=%fused_computation.32 | loop fusion | bytes 2359296 | tf_op jit(solution)/shard_map/stack | solution.py:79
  77.6 1.8 %copy.52 = f32[1,32,576]{2,1,0:T(8,128)} copy(f32[1,32,576]{1,2,0:T(8,128)} %get-tuple-element.12) | data formatting | bytes 147456 | tf_op jit(solution)/shard_map/stack | solution.py:79
  79.4 1.8 %copy.51 = f32[1,32,576]{2,1,0:T(8,128)} copy(f32[1,32,576]{1,2,0:T(8,128)} %get-tuple-element.13) | data formatting | bytes 147456 | tf_op jit(solution)/shard_map/stack | solution.py:79
  81.1 1.7 %copy.50 = f32[1,32,576]{2,1,0:T(8,128)} copy(f32[1,32,576]{1,2,0:T(8,128)} %get-tuple-element.14) | data formatting | bytes 147456 | tf_op jit(solution)/shard_map/stack | solution.py:79
  82.9 1.7 %copy.49 = f32[1,32,576]{2,1,0:T(8,128)} copy(f32[1,32,576]{1,2,0:T(8,128)} %get-tuple-element.15) | data formatting | bytes 147456 | tf_op jit(solution)/shard_map/stack | solution.py:79
  84.6 1.7 %copy.48 = f32[1,32,576]{2,1,0:T(8,128)} copy(f32[1,32,576]{1,2,0:T(8,128)} %get-tuple-element.16) | data formatting | bytes 147456 | tf_op jit(solution)/shard_map/stack | solution.py:79
  86.3 1.7 %copy.47 = f32[1,32,576]{2,1,0:T(8,128)} copy(f32[1,32,576]{1,2,0:T(8,128)} %get-tuple-element.17) | data formatting | bytes 147456 | tf_op jit(solution)/shard_map/stack | solution.py:79
  88.1 0.8 copy.46
  90.1 0.7 constant_dynamic-update-slice_fusion.15
  90.8 0.6 constant_dynamic-update-slice_fusion.14
  91.4 0.6 constant_dynamic-update-slice_fusion.13
  92.0 0.6 constant_dynamic-update-slice_fusion.12
  92.7 0.6 constant_dynamic-update-slice_fusion.11
  93.3 0.6 constant_dynamic-update-slice_fusion.10
  94.0 0.6 constant_dynamic-update-slice_fusion.9
  94.7 0.9 tile.5
  95.6 6.6 %all-to-all-start.4 = ((f32[16,32,256]{2,1,0:T(8,128)}), f32[16,32,256]{2,1,0:T(8,128)S(1)}, u32[]{:S(2)}, u32[]{:S(2)}) async-start(f32[16,32,256]{2,1,0:T(8,128)} %tile.5), calls=%async_computation.4 | async-start | bytes 1048576 | tf_op jit(solution)/shard_map/all_to_all | solution.py:56
  102.1 0.6 constant_dynamic-update-slice_fusion.8
  102.8 0.6 constant_dynamic-update-slice_fusion.7
  103.4 0.6 constant_dynamic-update-slice_fusion.6
  104.0 0.6 constant_dynamic-update-slice_fusion.5
  104.7 0.6 constant_dynamic-update-slice_fusion.4
  105.3 0.6 constant_dynamic-update-slice_fusion.3
  106.0 0.6 constant_dynamic-update-slice_fusion.2
  106.6 0.6 constant_dynamic-update-slice_fusion.1
  107.3 0.6 constant_dynamic-update-slice_fusion
  107.9 7.9 %all-to-all-done.4 = f32[16,32,256]{2,1,0:T(8,128)S(1)} async-done(((f32[16,32,256]{2,1,0:T(8,128)}), f32[16,32,256]{2,1,0:T(8,128)S(1)}, u32[]{:S(2)}, u32[]{:S(2)}) %all-to-all-start.4) | async-done | bytes 524320 | tf_op jit(solution)/shard_map/all_to_all | solution.py:56
  115.8 4.6 %all-to-all-start.2 = ((f32[16,32,576]{2,1,0:T(8,128)}), f32[16,32,576]{2,1,0:T(8,128)S(1)}, u32[]{:S(2)}, u32[]{:S(2)}) async-start(f32[16,32,576]{2,1,0:T(8,128)} %constant_dynamic-update-slice_fusion), calls=%async_computation.2 | async-start | bytes 2621440 | tf_op jit(solution)/shard_map/all_to_all | solution.py:78
  120.4 2.0 %collective-permute-start.5 = (f32[2,64]{1,0:T(2,128)S(1)}, f32[2,64]{1,0:T(2,128)S(1)}, u32[]{:S(2)}, u32[]{:S(2)}) collective-permute-start(f32[2,64]{1,0:T(2,128)S(1)} %bitcast.70), channel_id=1, source_target_pairs={{0,16},{16,0},{1,17},{17,1},{2,18},{18,2},{3,19},{19,3},{4,20},{20... | collective-permute-start | bytes 1544 | tf_op jit(solution)/shard_map/ppermute | solution.py:48
  122.5 0.8 collective-permute-done.5
  123.3 0.6 divide_subtract_fusion
  123.9 0.3 collective-permute-start.3
  124.2 1.0 convolution_bitcast_fusion
  125.5 25.1 %all-to-all-done.2 = f32[16,32,576]{2,1,0:T(8,128)S(1)} async-done(((f32[16,32,576]{2,1,0:T(8,128)}), f32[16,32,576]{2,1,0:T(8,128)S(1)}, u32[]{:S(2)}, u32[]{:S(2)}) %all-to-all-start.2) | async-done | bytes 1179680 | tf_op jit(solution)/shard_map/all_to_all | solution.py:78
  150.7 0.8 copy.53
  151.5 0.5 mul.135
  152.0 1.4 dynamic-slice_subtract_fusion
  153.4 2.6 %collective-permute-start.2 = (f32[32,9216]{1,0:T(8,128)S(1)}, f32[32,9216]{1,0:T(8,128)S(1)}, u32[]{:S(2)}, u32[]{:S(2)}) collective-permute-start(f32[32,9216]{1,0:T(8,128)S(1)} %dynamic-slice_subtract_fusion), channel_id=1, source_target_pairs={{0,16},{16,0},{1,17},{17,1},{2,18},{18,2},{3,19},{19,3},{4,20},{20... | collective-permute-start | bytes 3538952 | tf_op jit(solution)/shard_map/ppermute | solution.py:48
  156.0 0.7 multiply_reduce_fusion
  157.4 0.4 convolution_multiply_fusion.3
  157.8 0.4 multiply_subtract_fusion
  158.3 0.3 convolution_multiply_fusion.6
  158.5 0.3 fusion.10
  158.8 0.4 fusion.8
  159.2 0.4 fusion.7
  159.6 0.9 fusion.9
  160.5 1.6 maximum_select_fusion
  (53 shorter events, 1.7 us)
Async XLA Ops:
  0.6 2.2 %copy-start = (f32[64,256]{1,0:T(8,128)S(1)}, f32[64,256]{1,0:T(8,128)}, u32[]{:S(2)}) copy-start(f32[64,256]{1,0:T(8,128)} %param.12) | copy-start | bytes 196612
  2.0 8.3 %collective-permute-start = (f32[32,9216]{1,0:T(8,128)S(1)}, f32[32,9216]{1,0:T(8,128)S(1)}, u32[]{:S(2)}, u32[]{:S(2)}) collective-permute-start(f32[32,9216]{1,0:T(8,128)S(1)} %dynamic-slice_bitcast_fusion), channel_id=1, source_target_pairs={{0,16},{16,0},{1,17},{17,1},{2,18},{18,2},{3,19},{19,3},{4,20},{20... | collective-permute-start | bytes 3538952 | tf_op jit(solution)/shard_map/ppermute | solution.py:48
  3.6 20.6 %all-to-all-start = ((f32[16,32,256]{2,1,0:T(8,128)}), f32[16,32,256]{2,1,0:T(8,128)S(1)}, u32[]{:S(2)}, u32[]{:S(2)}) async-start(f32[16,32,256]{2,1,0:T(8,128)} %tile.4), calls=%async_computation | async-start | bytes 1048576 | tf_op jit(solution)/shard_map/all_to_all | solution.py:56
  24.2 35.0 %copy-start.3 = (f32[16,32,256]{2,1,0:T(8,128)}, f32[16,32,256]{2,1,0:T(8,128)S(1)}, u32[]{:S(2)}) copy-start(f32[16,32,256]{2,1,0:T(8,128)S(1)} %all-to-all-done) | copy-start | bytes 1572868
  61.5 3.6 %collective-permute-start.1 = (f32[576,256]{1,0:T(8,128)S(1)}, f32[576,256]{1,0:T(8,128)S(1)}, u32[]{:S(2)}, u32[]{:S(2)}) collective-permute-start(f32[576,256]{1,0:T(8,128)S(1)} %fusion.4), channel_id=1, source_target_pairs={{0,16},{16,0},{1,17},{17,1},{2,18},{18,2},{3,19},{19,3},{4,20},{20... | collective-permute-start | bytes 1769480 | tf_op jit(solution)/shard_map/ppermute | solution.py:48
  67.3 27.3 %all-to-all-start.3 = ((f32[16,32,256]{2,1,0:T(8,128)}), f32[16,32,256]{2,1,0:T(8,128)S(1)}, u32[]{:S(2)}, u32[]{:S(2)}) async-start(f32[16,32,256]{2,1,0:T(8,128)} %fusion), calls=%async_computation.3 | async-start | bytes 1048576 | tf_op jit(solution)/shard_map/all_to_all | solution.py:56
  71.5 2.3 %copy-start.4 = (f32[16,32,256]{2,1,0:T(8,128)S(1)}, f32[16,32,256]{2,1,0:T(8,128)}, u32[]{:S(2)}) copy-start(f32[16,32,256]{2,1,0:T(8,128)} %copy-done.3) | copy-start | bytes 1572868
  73.0 0.8 copy-start.2
  73.1 2.2 %copy-start.1 = (f32[576,256]{1,0:T(8,128)}, f32[576,256]{1,0:T(8,128)S(1)}, u32[]{:S(2)}) copy-start(f32[576,256]{1,0:T(8,128)S(1)} %get-tuple-element.28) | copy-start | bytes 1769476
  77.6 11.3 %copy-start.6 = (f32[1,32,576]{1,2,0:T(8,128)S(1)}, f32[1,32,576]{1,2,0:T(8,128)}, u32[]{:S(2)}) copy-start(f32[1,32,576]{1,2,0:T(8,128)} %get-tuple-element.19) | copy-start | bytes 221188
  79.3 9.6 %copy-start.5 = (f32[1,32,576]{1,2,0:T(8,128)S(1)}, f32[1,32,576]{1,2,0:T(8,128)}, u32[]{:S(2)}) copy-start(f32[1,32,576]{1,2,0:T(8,128)} %get-tuple-element.20) | copy-start | bytes 221188
  94.0 9.4 %copy-start.13 = (f32[1,32,576]{2,1,0:T(8,128)S(1)}, f32[1,32,576]{2,1,0:T(8,128)}, u32[]{:S(2)}) copy-start(f32[1,32,576]{2,1,0:T(8,128)} %copy.46) | copy-start | bytes 221188
  94.6 9.4 %copy-start.12 = (f32[1,32,576]{2,1,0:T(8,128)S(1)}, f32[1,32,576]{2,1,0:T(8,128)}, u32[]{:S(2)}) copy-start(f32[1,32,576]{2,1,0:T(8,128)} %copy.47) | copy-start | bytes 221188
  94.6 10.1 %copy-start.11 = (f32[1,32,576]{2,1,0:T(8,128)S(1)}, f32[1,32,576]{2,1,0:T(8,128)}, u32[]{:S(2)}) copy-start(f32[1,32,576]{2,1,0:T(8,128)} %copy.48) | copy-start | bytes 221188
  94.7 10.7 %copy-start.10 = (f32[1,32,576]{2,1,0:T(8,128)S(1)}, f32[1,32,576]{2,1,0:T(8,128)}, u32[]{:S(2)}) copy-start(f32[1,32,576]{2,1,0:T(8,128)} %copy.49) | copy-start | bytes 221188
  94.7 11.3 %copy-start.9 = (f32[1,32,576]{2,1,0:T(8,128)S(1)}, f32[1,32,576]{2,1,0:T(8,128)}, u32[]{:S(2)}) copy-start(f32[1,32,576]{2,1,0:T(8,128)} %copy.50) | copy-start | bytes 221188
  94.7 12.0 %copy-start.8 = (f32[1,32,576]{2,1,0:T(8,128)S(1)}, f32[1,32,576]{2,1,0:T(8,128)}, u32[]{:S(2)}) copy-start(f32[1,32,576]{2,1,0:T(8,128)} %copy.51) | copy-start | bytes 221188
  95.6 11.7 %copy-start.7 = (f32[1,32,576]{2,1,0:T(8,128)S(1)}, f32[1,32,576]{2,1,0:T(8,128)}, u32[]{:S(2)}) copy-start(f32[1,32,576]{2,1,0:T(8,128)} %copy.52) | copy-start | bytes 221188
  95.6 20.2 %all-to-all-start.4 = ((f32[16,32,256]{2,1,0:T(8,128)}), f32[16,32,256]{2,1,0:T(8,128)S(1)}, u32[]{:S(2)}, u32[]{:S(2)}) async-start(f32[16,32,256]{2,1,0:T(8,128)} %tile.5), calls=%async_computation.4 | async-start | bytes 1048576 | tf_op jit(solution)/shard_map/all_to_all | solution.py:56
  107.9 12.5 %copy-start.15 = (f32[1,2,64]{2,1,0:T(2,128)S(1)}, f32[1,2,64]{2,1,0:T(2,128)}, u32[]{:S(2)}) copy-start(f32[1,2,64]{2,1,0:T(2,128)} %param.10) | copy-start | bytes 1540
  107.9 15.4 %copy-start.14 = (f32[2,64]{1,0:T(2,128)S(1)}, f32[2,64]{1,0:T(2,128)}, u32[]{:S(2)}) copy-start(f32[2,64]{1,0:T(2,128)} %param.15) | copy-start | bytes 1540
  107.9 15.4 %copy-start.16 = (f32[2,64]{1,0:T(2,128)S(1)}, f32[2,64]{1,0:T(2,128)}, u32[]{:S(2)}) copy-start(f32[2,64]{1,0:T(2,128)} %param.16) | copy-start | bytes 1540
  107.9 15.4 %copy-start.17 = (f32[2,64]{1,0:T(2,128)S(1)}, f32[2,64]{1,0:T(2,128)}, u32[]{:S(2)}) copy-start(f32[2,64]{1,0:T(2,128)} %param.17) | copy-start | bytes 1540
  115.8 34.8 %all-to-all-start.2 = ((f32[16,32,576]{2,1,0:T(8,128)}), f32[16,32,576]{2,1,0:T(8,128)S(1)}, u32[]{:S(2)}, u32[]{:S(2)}) async-start(f32[16,32,576]{2,1,0:T(8,128)} %constant_dynamic-update-slice_fusion), calls=%async_computation.2 | async-start | bytes 2621440 | tf_op jit(solution)/shard_map/all_to_all | solution.py:78
  120.4 2.8 %collective-permute-start.5 = (f32[2,64]{1,0:T(2,128)S(1)}, f32[2,64]{1,0:T(2,128)S(1)}, u32[]{:S(2)}, u32[]{:S(2)}) collective-permute-start(f32[2,64]{1,0:T(2,128)S(1)} %bitcast.70), channel_id=1, source_target_pairs={{0,16},{16,0},{1,17},{17,1},{2,18},{18,2},{3,19},{19,3},{4,20},{20... | collective-permute-start | bytes 1544 | tf_op jit(solution)/shard_map/ppermute | solution.py:48
  123.9 34.4 %collective-permute-start.3 = (f32[32,256]{1,0:T(8,128)S(1)}, f32[32,256]{1,0:T(8,128)S(1)}, u32[]{:S(2)}, u32[]{:S(2)}) collective-permute-start(f32[32,256]{1,0:T(8,128)S(1)} %reduce_sum.18), channel_id=1, source_target_pairs={{0,16},{16,0},{1,17},{17,1},{2,18},{18,2},{3,19},{19,3},{4,20},{20... | collective-permute-start | bytes 98312 | tf_op jit(solution)/shard_map/ppermute | solution.py:48
  125.3 30.8 %collective-permute-start.4 = (f32[256,256]{1,0:T(8,128)S(1)}, f32[256,256]{1,0:T(8,128)S(1)}, u32[]{:S(2)}, u32[]{:S(2)}) collective-permute-start(f32[256,256]{1,0:T(8,128)S(1)} %convolution_bitcast_fusion), channel_id=1, source_target_pairs={{0,16},{16,0},{1,17},{17,1},{2,18},{18,2},{3,19},{19,3},{4,20},{20... | collective-permute-start | bytes 786440 | tf_op jit(solution)/shard_map/ppermute | solution.py:48
  153.4 7.1 %collective-permute-start.2 = (f32[32,9216]{1,0:T(8,128)S(1)}, f32[32,9216]{1,0:T(8,128)S(1)}, u32[]{:S(2)}, u32[]{:S(2)}) collective-permute-start(f32[32,9216]{1,0:T(8,128)S(1)} %dynamic-slice_subtract_fusion), channel_id=1, source_target_pairs={{0,16},{16,0},{1,17},{17,1},{2,18},{18,2},{3,19},{19,3},{4,20},{20... | collective-permute-start | bytes 3538952 | tf_op jit(solution)/shard_map/ppermute | solution.py:48
